TPU v7x, 256 devices: a whole 4x4x8 slice. The times are simulated.
256 devices in a mesh: feat: 8 (over z), dom: 32 (over x, y, core).
Axes of the slice: x: 4, y: 4, z: 8, core: 2. Of those that a mesh axis runs over, the one named last changes fastest.
Arguments:
- features: bfloat16 [128, 32768], P('feat', 'dom'), may hold values from -6 to 6
- self_weight: bfloat16 [128, 512], P('feat'), may hold values from -0.5 to 0.5
- neighbor_weight: bfloat16 [128, 512], P('feat'), may hold values from -0.5 to 0.5
- unit_bias: float32 [512], P('feat'), may hold values from -3 to 3
- send_blocks: int32 [32, 32, 4], P('dom'), may hold values from 0 to 7
- send_counts: int32 [32, 32], P('dom'), may hold values from 0 to 4, as said below
- tile_target: int32 [32, 256], P('dom'), may hold values from 0 to 7
- tile_source: int32 [32, 256], P('dom'), may hold values from 0 to 135, as said below
- tile_count: int32 [32], P('dom'), may hold values from 64 to 256, as said below
- tile_weights: bfloat16 [32, 256, 128, 128], P('dom'), may hold values from 0 to 1, as said below
- out_grad: bfloat16 [512, 32768], P('feat', 'dom'), may hold values from -0.119628906 to 0.119628906
Outputs:
- hidden: bfloat16 [512, 32768], P('feat', 'dom')
- self_gradient: float32 [128, 512], P('feat')
- neighbor_gradient: float32 [128, 512], P('feat')
- bias_gradient: float32 [512], P('feat')
Inputs may be any that keep to these rules, and one draw needn't show every extreme that they name: `send_counts`: the diagonal is 0; each partition d fills all 4 slots toward partitions d - 1 and d + 1 (counted round). `tile_count`: at least one partition has all 256 tiles live. `tile_source`: tile 0 of partition d reads slot 8 + ((d + 1) mod 32) * 4, tile 1 reads slot 8 + ((d - 1) mod 32) * 4. `tile_weights`: entries may be 0.
All inputs are finite; a program needn't handle non-finite values.
Results may differ from a plain program's by a relative error of at most 0.005.
Values may be sent and summed in bfloat16 or wider, within the bound.
A program may use at most 64 MiB of HBM per device.

v0:
```python
import jax
import jax.numpy as jnp
from jax import lax
from jax.sharding import PartitionSpec as P

BLK = 128
BMAX = 4


def activate(values):
    return jax.nn.gelu(values, approximate=True)


def body(
    features,
    self_weight,
    neighbor_weight,
    unit_bias,
    send_blocks,
    send_counts,
    tile_target,
    tile_source,
    tile_count,
    tile_weights,
    out_grad,
):
    row_count = features.shape[1]
    unit_width = out_grad.shape[0]
    own_blocks = row_count // BLK
    neighbor_term = jnp.einsum(
        "fh,fr->hr", neighbor_weight, features, preferred_element_type=jnp.float32
    )
    self_term = jnp.einsum("fh,fr->hr", self_weight, features, preferred_element_type=jnp.float32)
    stacked = lax.psum_scatter(
        jnp.concatenate([neighbor_term, self_term], axis=1), "feat", scatter_dimension=0, tiled=True
    )
    projected = stacked[:, :row_count].astype(jnp.bfloat16)
    self_part = stacked[:, row_count:]
    slot_index = jnp.arange(BMAX, dtype=jnp.int32)
    chosen = send_blocks[0].reshape(-1)
    live_slots = (slot_index[None, :] < send_counts[0][:, None]).reshape(-1)
    own_table = projected.reshape(unit_width, own_blocks, BLK)
    outgoing = jnp.take(own_table, chosen, axis=1) * live_slots.astype(jnp.bfloat16)[None, :, None]
    incoming = lax.all_to_all(
        outgoing.reshape(unit_width, -1), "dom", split_axis=1, concat_axis=1, tiled=True
    )
    slot_table = jnp.concatenate([projected, incoming], axis=1).reshape(unit_width, -1, BLK)
    slot_number = slot_table.shape[1]
    weights = tile_weights[0]
    tile_total = weights.shape[0]
    live_tiles = (jnp.arange(tile_total, dtype=jnp.int32) < tile_count[0]).astype(jnp.float32)
    sources = tile_source[0]
    targets = tile_target[0]
    picked = jnp.take(slot_table, sources, axis=1)
    products = (
        jnp.einsum("htc,trc->thr", picked, weights, preferred_element_type=jnp.float32)
        * live_tiles[:, None, None]
    )
    block_sums = jax.ops.segment_sum(products, targets, num_segments=own_blocks)
    aggregate = jnp.transpose(block_sums, (1, 0, 2)).reshape(unit_width, row_count)
    unit_ones = jnp.ones((weights.shape[2],), jnp.bfloat16)
    row_sums = (
        jnp.einsum("trc,c->tr", weights, unit_ones, preferred_element_type=jnp.float32)
        * live_tiles[:, None]
    )
    degree = 1.0 + jax.ops.segment_sum(row_sums, targets, num_segments=own_blocks).reshape(
        row_count
    )
    summed_input = self_part + aggregate / degree[None, :] + unit_bias[:, None]
    hidden, pullback = jax.vjp(activate, summed_input)
    summed_grad = pullback(out_grad.astype(jnp.float32))[0]
    scaled = (summed_grad / degree[None, :]).astype(jnp.bfloat16)
    target_rows = jnp.take(scaled.reshape(unit_width, own_blocks, BLK), targets, axis=1)
    pushed = (
        jnp.einsum("htr,trc->thc", target_rows, weights, preferred_element_type=jnp.float32)
        * live_tiles[:, None, None]
    )
    slot_totals = jax.ops.segment_sum(pushed, sources, num_segments=slot_number)
    returned = lax.all_to_all(
        slot_totals[own_blocks:], "dom", split_axis=0, concat_axis=0, tiled=True
    )
    returned = returned * live_slots.astype(jnp.float32)[:, None, None]
    folded = (
        jax.ops.segment_sum(returned, chosen, num_segments=own_blocks) + slot_totals[:own_blocks]
    )
    neighbor_totals = (
        jnp.transpose(folded, (1, 0, 2)).reshape(unit_width, row_count).astype(jnp.bfloat16)
    )
    narrow_total = summed_grad.astype(jnp.bfloat16)
    bias_part = jnp.sum(summed_grad, axis=1)
    full_narrow, full_neighbor = (
        lax.all_gather(narrow_total, "feat", axis=0, tiled=True),
        lax.all_gather(neighbor_totals, "feat", axis=0, tiled=True),
    )
    self_term = jnp.einsum("fr,hr->fh", features, full_narrow, preferred_element_type=jnp.float32)
    neighbor_term = jnp.einsum(
        "fr,hr->fh", features, full_neighbor, preferred_element_type=jnp.float32
    )
    self_gradient, neighbor_gradient, bias_gradient = lax.psum(
        (self_term, neighbor_term, bias_part), "dom"
    )
    return (hidden.astype(jnp.bfloat16), self_gradient, neighbor_gradient, bias_gradient)


def solution(mesh):
    in_specs = (
        P("feat", "dom"),
        P("feat", None),
        P("feat", None),
        P("feat"),
        P("dom", None, None),
        P("dom", None),
        P("dom", None),
        P("dom", None),
        P("dom"),
        P("dom", None, None, None),
        P("feat", "dom"),
    )
    out_specs = (P("feat", "dom"), P("feat", None), P("feat", None), P("feat"))
    return jax.shard_map(body, mesh=mesh, in_specs=in_specs, out_specs=out_specs, check_vma=False)
```

profile of v0, /device:TPU:1, one launch (start us, length us, event | category | flops | bytes accessed | tf_op | source)
XLA Modules:
  0.0 458.1 jit_solution(16673961788908352427)
XLA Ops:
  7.2 0.0 copy-start
  7.2 0.0 reduce-scatter.2.cloned.1.call-start
  7.2 0.7 copy-done
  7.9 1.2 fusion.48
  9.1 1.2 fusion.47
  10.3 2.4 pad_maximum_fusion
  12.7 0.0 reduce-scatter.2.cloned.1.call-update
  12.7 0.7 copy-done.4
  13.4 0.1 copy.44
  13.5 0.1 copy.43
  13.6 0.1 broadcast_in_dim.51
  13.7 0.1 reshape_squeeze.6
  13.8 0.0 copy-done.7
  13.8 0.1 fusion.37
  13.9 0.1 mul.88
  14.1 58.0 %reduce-scatter.2.cloned.1.call-done = f32[64,2048]{1,0:T(8,128)} async-done(((f32[512,2048]{1,0:T(8,128)}), f32[64,2048]{1,0:T(8,128)}) %reduce-scatter.2.cloned.1.call-update) | async-done | bytes 524304 | tf_op jit(solution)/shard_map/reduce_scatter | solution.py:34
  72.1 1.0 copy_bitcast_fusion.3
  73.0 1.0 gather_fusion
  74.0 2.7 copy.46
  76.7 3.1 gather.15
  79.8 0.2 select_multiply_fusion
  80.0 0.0 copy-start.3
  80.0 2.5 copy.47
  82.5 7.5 %all-to-all-start = ((bf16[64,32,512]{2,0,1:T(8,128)(2,1)}), bf16[64,32,512]{2,0,1:T(8,128)(2,1)S(1)}, u32[]{:S(2)}, u32[]{:S(2)}) async-start(bf16[64,32,512]{2,0,1:T(8,128)(2,1)} %copy.47), calls=%async_computation.1 | async-start | bytes 4194304 | tf_op jit(solution)/shard_map/all_to_all | solution.py:44
  90.7 0.0 copy-start.5
  90.7 5.7 %fusion.2 = f32[1,256,128]{2,0,1:T(1,128)S(1)} fusion(bf16[1,256,128,128]{3,2,1,0:T(8,128)(2,1)} %param.20), kind=kOutput, calls=%fused_computation.9 | convolution fusion | flops 8388608 | bytes 8519680 | tf_op jit(solution)/shard_map/trc,c->tr/dot_general | solution.py:63
  96.4 2.2 scatter_custom_fusion.1
  98.7 19.6 %all-to-all-done = bf16[64,32,512]{2,0,1:T(8,128)(2,1)S(1)} async-done(((bf16[64,32,512]{2,0,1:T(8,128)(2,1)}), bf16[64,32,512]{2,0,1:T(8,128)(2,1)S(1)}, u32[]{:S(2)}, u32[]{:S(2)}) %all-to-all-start) | async-done | bytes 2097184 | tf_op jit(solution)/shard_map/all_to_all | solution.py:44
  118.3 0.2 copy.58
  118.5 0.6 copy_bitcast_fusion
  119.1 3.1 gather_fusion.1
  122.2 13.6 %broadcast_multiply_fusion.1 = f32[256,64,128]{2,1,0:T(8,128)} fusion(f32[256]{0:T(256)S(1)} %get-tuple-element.14, bf16[1,256,128,128]{3,2,1,0:T(8,128)(2,1)} %param.20, bf16[256,64,128]{2,1,0:T(8,128)(2,1)} %gather_fusion.1, pred[256]{0:T(512)(128)(4,1)S(1)} %get-tuple-element.15), kind=kOutput, calls=%fused_computation.19 | convolution fusion | flops 541065216 | bytes 20972800 | tf_op jit(solution)/shard_map/htc,trc->thr/dot_general | solution.py:56
  135.8 0.0 copy-start.2
  135.8 0.0 copy-start.6
  135.9 26.2 %scatter_fusion = f32[8,64,128]{2,1,0:T(8,128)S(1)} fusion(f32[8,64,128]{2,1,0:T(8,128)S(1)} %broadcast.124, s32[256]{0:T(256)S(1)} %bitcast.115, f32[256,64,128]{2,1,0:T(8,128)} %broadcast_multiply_fusion.1), kind=kCustom, calls=%fused_computation.3 | custom fusion | flops 2097152 | bytes 25166848 | tf_op jit(solution)/shard_map/scatter-add | solution.py:59
  162.1 1.6 fusion.45
  163.7 0.7 fusion.35
  164.4 3.1 gather_fusion.2
  167.4 10.3 %broadcast_multiply_fusion = f32[256,64,128]{2,1,0:T(8,128)} fusion(f32[256]{0:T(256)S(1)} %get-tuple-element.14, bf16[1,256,128,128]{3,2,1,0:T(8,128)(2,1)} %param.20, bf16[256,64,128]{2,1,0:T(8,128)(2,1)} %gather_fusion.2, pred[256]{0:T(512)(128)(4,1)S(1)} %compare_and_fusion), kind=kOutput, calls=%fused_computation.18 | convolution fusion | flops 541065216 | bytes 20972800 | tf_op jit(solution)/shard_map/htr,trc->thc/dot_general | solution.py:75
  177.8 2.6 broadcast_in_dim.58
  180.4 39.3 %scatter_fusion.1 = f32[136,64,128]{2,1,0:T(8,128)} fusion(f32[136,64,128]{2,1,0:T(8,128)} %broadcast_in_dim.58, s32[256]{0:T(256)S(1)} %bitcast.112, f32[256,64,128]{2,1,0:T(8,128)} %broadcast_multiply_fusion), kind=kCustom, calls=%fused_computation.5 | custom fusion | flops 2097152 | bytes 25166848 | tf_op jit(solution)/shard_map/scatter-add | solution.py:78
  219.8 4.7 %slice.26 = f32[128,64,128]{2,1,0:T(8,128)} slice(f32[136,64,128]{2,1,0:T(8,128)} %scatter_fusion.1), slice={[8:136], [0:64], [0:128]} | slice | bytes 8388608 | tf_op jit(solution)/shard_map/slice | solution.py:80
  224.5 5.3 %all-to-all-start.1 = ((f32[128,64,128]{2,1,0:T(8,128)}), f32[128,64,128]{2,1,0:T(8,128)}, u32[]{:S(2)}, u32[]{:S(2)}) async-start(f32[128,64,128]{2,1,0:T(8,128)} %slice.26), calls=%async_computation.2 | async-start | bytes 8388608 | tf_op jit(solution)/shard_map/all_to_all | solution.py:79
  229.8 0.0 all-gather.3.cloned.1.call-start
  229.9 0.7 all-gather.3.cloned.1.call-update
  230.6 0.0 all-gather.5.cloned.1.call-start
  230.6 0.1 reshape.247
  230.7 0.1 reshape.196
  230.8 1.0 slice.25
  231.8 50.3 %all-to-all-done.1 = f32[128,64,128]{2,1,0:T(8,128)} async-done(((f32[128,64,128]{2,1,0:T(8,128)}), f32[128,64,128]{2,1,0:T(8,128)}, u32[]{:S(2)}, u32[]{:S(2)}) %all-to-all-start.1) | async-done | bytes 4194336 | tf_op jit(solution)/shard_map/all_to_all | solution.py:79
  282.1 4.5 broadcast_multiply_fusion.2
  286.6 13.5 %scatter_fusion.2 = f32[8,64,128]{2,1,0:T(8,128)S(1)} fusion(f32[8,64,128]{2,1,0:T(8,128)S(1)} %slice.25, s32[128]{0:T(128)S(1)} %reshape.247, f32[128,64,128]{2,1,0:T(8,128)} %broadcast_multiply_fusion.2), kind=kCustom, calls=%fused_computation.6 | custom fusion | flops 1048576 | bytes 12583424 | tf_op jit(solution)/shard_map/scatter-add | solution.py:84
  300.2 0.7 copy_bitcast_fusion.1
  300.8 0.0 all-gather.5.cloned.1.call-update
  300.9 0.0 all-reduce.3.cloned.1.call-start
  300.9 0.0 all-gather.3.cloned.1.call-done
  300.9 2.2 convolution_bitcast_fusion.1
  303.2 29.7 %all-gather.5.cloned.1.call-done = bf16[512,1024]{1,0:T(8,128)(2,1)} async-done(((bf16[64,1024]{1,0:T(8,128)(2,1)}), bf16[512,1024]{1,0:T(8,128)(2,1)}) %all-gather.5.cloned.1.call-update) | async-done | bytes 1048592 | tf_op jit(solution)/shard_map/all_gather | solution.py:93
  332.9 2.2 convolution_bitcast_fusion
  335.1 0.0 all-reduce.3.cloned.1.call-update
  335.1 112.6 %all-reduce.3.cloned.1.call-done = (f32[16,512]{1,0:T(8,128)}, f32[16,512]{1,0:T(8,128)}, f32[64]{0:T(128)}) async-done(((f32[16,512]{1,0:T(8,128)}, f32[16,512]{1,0:T(8,128)}, f32[64]{0:T(128)}), (f32[16,512]{1,0:T(8,128)}, f32[16,512]{1,0:T(8,128)}, f32[64]{0:T(128)})) %all-reduce.3.cloned.1.call-update) | async-done | bytes 65808 | tf_op jit(solution)/shard_map/psum | solution.py:99
  447.7 1.4 copy.85
  449.1 1.4 copy.86
  450.4 1.1 copy.87
  (22 shorter events, 0.1 us)
Async XLA Ops:
  7.2 0.8 copy-start
  7.2 64.9 %reduce-scatter.2.cloned.1.call-start = ((), (), s32[]{:S(2)}) async-start(), calls=%async_computation.3 | async-start | bytes 4718592 | tf_op jit(solution)/shard_map/reduce_scatter | solution.py:34
  12.7 0.7 copy-start.4
  12.7 1.1 copy-start.7
  80.0 10.6 %copy-start.3 = (s32[1,256]{1,0:T(1,128)S(1)}, s32[1,256]{1,0:T(1,128)}, u32[]{:S(2)}) copy-start(s32[1,256]{1,0:T(1,128)} %param.18) | copy-start | bytes 3076
  82.5 35.8 %all-to-all-start = ((bf16[64,32,512]{2,0,1:T(8,128)(2,1)}), bf16[64,32,512]{2,0,1:T(8,128)(2,1)S(1)}, u32[]{:S(2)}, u32[]{:S(2)}) async-start(bf16[64,32,512]{2,0,1:T(8,128)(2,1)} %copy.47), calls=%async_computation.1 | async-start | bytes 4194304 | tf_op jit(solution)/shard_map/all_to_all | solution.py:44
  90.7 5.7 %copy-start.5 = (s32[1,256]{1,0:T(1,128)S(1)}, s32[1,256]{1,0:T(1,128)}, u32[]{:S(2)}) copy-start(s32[1,256]{1,0:T(1,128)} %param.17) | copy-start | bytes 3076
  90.7 8.0 %copy-start.1 = (f32[64,2048]{1,0:T(8,128)S(1)}, f32[64,2048]{1,0:T(8,128)}, u32[]{:S(2)}) copy-start(f32[64,2048]{1,0:T(8,128)} %reduce-scatter.2.cloned.1.call-done) | copy-start | bytes 1572868
  135.8 26.3 %copy-start.2 = (bf16[64,1024]{1,0:T(8,128)(2,1)S(1)}, bf16[64,1024]{1,0:T(8,128)(2,1)}, u32[]{:S(2)}) copy-start(bf16[64,1024]{1,0:T(8,128)(2,1)} %param.21) | copy-start | bytes 393220
  135.8 26.3 %copy-start.6 = (f32[64]{0:T(128)S(1)}, f32[64]{0:T(128)}, u32[]{:S(2)}) copy-start(f32[64]{0:T(128)} %param.14) | copy-start | bytes 772
  224.5 57.6 %all-to-all-start.1 = ((f32[128,64,128]{2,1,0:T(8,128)}), f32[128,64,128]{2,1,0:T(8,128)}, u32[]{:S(2)}, u32[]{:S(2)}) async-start(f32[128,64,128]{2,1,0:T(8,128)} %slice.26), calls=%async_computation.2 | async-start | bytes 8388608 | tf_op jit(solution)/shard_map/all_to_all | solution.py:79
  229.8 71.1 %all-gather.3.cloned.1.call-start = ((), (), s32[]{:S(2)}) async-start(), calls=%async_computation.4 | async-start | bytes 1179648 | tf_op jit(solution)/shard_map/all_gather | solution.py:92
  230.6 102.3 %all-gather.5.cloned.1.call-start = ((), (), s32[]{:S(2)}) async-start(), calls=%async_computation.5 | async-start | bytes 1179648 | tf_op jit(solution)/shard_map/all_gather | solution.py:93
  300.9 146.8 %all-reduce.3.cloned.1.call-start = ((), (), s32[]{:S(2)}) async-start(), calls=%async_computation.6 | async-start | bytes 132096 | tf_op jit(solution)/shard_map/psum | solution.py:99
Sparse Core Ops, SparseCore 0:
  12.9 59.1 reduce-scatter.1
  232.4 33.6 all-gather.2
  301.0 31.8 all-gather.4
  336.9 110.7 all-reduce.2
where the time goes:
time: 460 us; the launch traced here: 458 us
  waiting for transfers between devices  271 us (59%)
  other arithmetic  92.1 us (20%)
  matrix products  36.5 us (8%)
  local copies, waits for them, and re-layouts  30.9 us (7%)
  between operations  14.7 us (3%)
  starting transfers between devices  12.9 us (3%)
    psum x1, waiting for transfers between devices, body(): lax.psum((self_term, neighbor_term, bias_part), 'dom')  113 us
    reduce_scatter x1, waiting for transfers between devices, body(): lax.psum_scatter(jnp.concatenate([neighbor_term, self_term], axis=1), 'fe...  58 us
    all_to_all x1, waiting for transfers between devices, body(): lax.all_to_all(slot_totals[own_blocks:], 'dom', split_axis=0, concat_axis...  50.3 us
    scatter-add x1, other arithmetic, body(): slot_totals = jax.ops.segment_sum(pushed, sources, num_segments=slot_number)  39.3 us
    all_gather x1, waiting for transfers between devices, body(): lax.all_gather(neighbor_totals, 'feat', axis=0, tiled=True)  29.7 us
    scatter-add x1, other arithmetic, body(): block_sums = jax.ops.segment_sum(products, targets, num_segments=own_blocks)  26.2 us
    all_to_all x1, waiting for transfers between devices, body(): lax.all_to_all(outgoing.reshape(unit_width, -1), 'dom', split_axis=1, con...  19.6 us
    dot_general x1, matrix products, body(): jnp.einsum('htc,trc->thr', picked, weights, preferred_element_type=jnp.fl...  13.6 us
  transfers between devices with their start and end apart: 6, of which 5 were waited for; matrix products, arithmetic and copies ran while one was open for 7% of the time, Pallas kernels for 0%

commit v1 on v0

--- a/solution.py
+++ b/solution.py
@@ -41,8 +41,14 @@
     live_slots = (slot_index[None, :] < send_counts[0][:, None]).reshape(-1)
     own_table = projected.reshape(unit_width, own_blocks, BLK)
     outgoing = jnp.take(own_table, chosen, axis=1) * live_slots.astype(jnp.bfloat16)[None, :, None]
-    incoming = lax.all_to_all(
-        outgoing.reshape(unit_width, -1), "dom", split_axis=1, concat_axis=1, tiled=True
+    incoming = jnp.concatenate(
+        lax.all_to_all(
+            jnp.stack(jnp.split(outgoing.reshape(unit_width, -1), lax.axis_size("dom"), axis=1)),
+            "dom",
+            0,
+            0,
+        ),
+        axis=1,
     )
     slot_table = jnp.concatenate([projected, incoming], axis=1).reshape(unit_width, -1, BLK)
     slot_number = slot_table.shape[1]

time: 460 us -> 472 us (1.026)
  local copies, waits for them, and re-layouts: 30.9 us -> 42.5 us
    unnamed x22 -> x53, local copies, waits for them, and re-layouts: 5.37 us -> 24.7 us
    gather x3 -> x1, local copies, waits for them, and re-layouts: 6.74 us -> 0.95 us  [body(): jnp.take(own_table, chosen, axis=1)]
where the time goes in v1:
time: 472 us; the launch traced here: 470 us
  waiting for transfers between devices  271 us (57%)
  other arithmetic  92.4 us (20%)
  local copies, waits for them, and re-layouts  42.5 us (9%)
  matrix products  35.7 us (8%)
  between operations  14.7 us (3%)
  starting transfers between devices  13.1 us (3%)
    psum x1, waiting for transfers between devices, body(): lax.psum((self_term, neighbor_term, bias_part), 'dom')  113 us
    reduce_scatter x1, waiting for transfers between devices, body(): lax.psum_scatter(jnp.concatenate([neighbor_term, self_term], axis=1), 'fe...  58 us
    all_to_all x1, waiting for transfers between devices, body(): lax.all_to_all(slot_totals[own_blocks:], 'dom', split_axis=0, concat_axis...  50.4 us
    scatter-add x1, other arithmetic, body(): slot_totals = jax.ops.segment_sum(pushed, sources, num_segments=slot_number)  39.3 us
    all_gather x1, waiting for transfers between devices, body(): lax.all_gather(neighbor_totals, 'feat', axis=0, tiled=True)  29.7 us
    scatter-add x1, other arithmetic, body(): block_sums = jax.ops.segment_sum(products, targets, num_segments=own_blocks)  26.2 us
    unnamed x53, local copies, waits for them, and re-layouts  24.7 us
    all_to_all x1, waiting for transfers between devices, body(): lax.all_to_all(jnp.stack(jnp.split(outgoing.reshape(unit_width, -1), lax....  19.6 us
  transfers between devices with their start and end apart: 6, of which 5 were waited for; matrix products, arithmetic and copies ran while one was open for 7% of the time, Pallas kernels for 0%

profile of v1, /device:TPU:1, one launch (start us, length us, event | category | flops | bytes accessed | tf_op | source)
XLA Modules:
  0.0 469.5 jit_solution(14351609828327084360)
XLA Ops:
  7.2 0.7 copy-done
  7.9 1.2 fusion.81
  9.6 2.5 pad_maximum_fusion
  12.0 0.7 copy-done.6
  13.4 58.0 %reduce-scatter.2.cloned.1.call-done = f32[64,2048]{1,0:T(8,128)} async-done(((f32[512,2048]{1,0:T(8,128)}), f32[64,2048]{1,0:T(8,128)}) %reduce-scatter.2.cloned.1.call-update) | async-done | bytes 524304 | tf_op jit(solution)/shard_map/reduce_scatter | solution.py:34
  71.4 1.0 copy_bitcast_fusion.3
  72.3 1.0 gather_fusion
  73.8 0.6 fusion.68
  74.5 0.6 fusion.67
  75.1 0.6 fusion.66
  75.7 0.6 fusion.65
  76.3 0.6 fusion.64
  77.0 0.6 fusion.63
  77.6 0.6 fusion.62
  78.2 0.6 fusion.61
  78.8 0.6 fusion.60
  79.5 0.6 fusion.59
  80.1 0.6 fusion.58
  80.7 0.6 fusion.57
  81.3 0.6 fusion.56
  82.0 0.6 fusion.55
  82.6 0.6 fusion.54
  83.2 0.6 fusion.53
  83.8 0.6 fusion.52
  85.1 0.6 fusion.50
  85.7 0.6 fusion.49
  86.3 0.6 fusion.48
  86.9 0.6 fusion.47
  87.6 0.6 fusion.46
  88.8 0.6 fusion.44
  89.4 0.6 fusion.43
  90.0 0.6 fusion.42
  90.7 0.6 fusion.41
  91.3 0.6 fusion.40
  91.9 0.6 fusion.39
  93.8 7.6 %all-to-all-start = ((bf16[32,64,512]{2,1,0:T(8,128)(2,1)}), bf16[32,64,512]{2,1,0:T(8,128)(2,1)S(1)}, u32[]{:S(2)}, u32[]{:S(2)}) async-start(bf16[32,64,512]{2,1,0:T(8,128)(2,1)} %fusion.37), calls=%async_computation.1 | async-start | bytes 4194304 | tf_op jit(solution)/shard_map/all_to_all | solution.py:45
  102.1 5.7 %fusion.2 = f32[1,256,128]{2,0,1:T(1,128)S(1)} fusion(bf16[1,256,128,128]{3,2,1,0:T(8,128)(2,1)} %param.20), kind=kOutput, calls=%fused_computation.9 | convolution fusion | flops 8388608 | bytes 8519680 | tf_op jit(solution)/shard_map/trc,c->tr/dot_general | solution.py:69
  107.8 2.2 scatter_custom_fusion.1
  110.1 19.6 %all-to-all-done = bf16[32,64,512]{2,1,0:T(8,128)(2,1)S(1)} async-done(((bf16[32,64,512]{2,1,0:T(8,128)(2,1)}), bf16[32,64,512]{2,1,0:T(8,128)(2,1)S(1)}, u32[]{:S(2)}, u32[]{:S(2)}) %all-to-all-start) | async-done | bytes 2097184 | tf_op jit(solution)/shard_map/all_to_all | solution.py:45
  129.9 0.6 copy_bitcast_fusion
  130.5 3.1 gather_fusion.1
  133.6 13.6 %broadcast_multiply_fusion.1 = f32[256,64,128]{2,1,0:T(8,128)} fusion(f32[256]{0:T(256)S(1)} %get-tuple-element.16, bf16[1,256,128,128]{3,2,1,0:T(8,128)(2,1)} %param.20, bf16[256,64,128]{2,1,0:T(8,128)(2,1)} %gather_fusion.1, pred[256]{0:T(512)(128)(4,1)S(1)} %get-tuple-element.17), kind=kOutput, calls=%fused_computation.19 | convolution fusion | flops 541065216 | bytes 20972800 | tf_op jit(solution)/shard_map/htc,trc->thr/dot_general | solution.py:62
  147.2 26.2 %scatter_fusion = f32[8,64,128]{2,1,0:T(8,128)S(1)} fusion(f32[8,64,128]{2,1,0:T(8,128)S(1)} %broadcast.113, s32[256]{0:T(256)S(1)} %bitcast.238, f32[256,64,128]{2,1,0:T(8,128)} %broadcast_multiply_fusion.1), kind=kCustom, calls=%fused_computation.3 | custom fusion | flops 2097152 | bytes 25166848 | tf_op jit(solution)/shard_map/scatter-add | solution.py:65
  173.5 1.6 fusion.78
  175.1 0.7 fusion.36
  175.8 3.1 gather_fusion.2
  178.8 10.3 %broadcast_multiply_fusion = f32[256,64,128]{2,1,0:T(8,128)} fusion(f32[256]{0:T(256)S(1)} %get-tuple-element.16, bf16[1,256,128,128]{3,2,1,0:T(8,128)(2,1)} %param.20, bf16[256,64,128]{2,1,0:T(8,128)(2,1)} %gather_fusion.2, pred[256]{0:T(512)(128)(4,1)S(1)} %compare_and_fusion), kind=kOutput, calls=%fused_computation.18 | convolution fusion | flops 541065216 | bytes 20972800 | tf_op jit(solution)/shard_map/htr,trc->thc/dot_general | solution.py:81
  189.2 2.6 broadcast_in_dim.58
  191.8 39.3 %scatter_fusion.1 = f32[136,64,128]{2,1,0:T(8,128)} fusion(f32[136,64,128]{2,1,0:T(8,128)} %broadcast_in_dim.58, s32[256]{0:T(256)S(1)} %bitcast.235, f32[256,64,128]{2,1,0:T(8,128)} %broadcast_multiply_fusion), kind=kCustom, calls=%fused_computation.5 | custom fusion | flops 2097152 | bytes 25166848 | tf_op jit(solution)/shard_map/scatter-add | solution.py:84
  231.1 4.7 %slice.26 = f32[128,64,128]{2,1,0:T(8,128)} slice(f32[136,64,128]{2,1,0:T(8,128)} %scatter_fusion.1), slice={[8:136], [0:64], [0:128]} | slice | bytes 8388608 | tf_op jit(solution)/shard_map/slice | solution.py:86
  235.8 5.4 %all-to-all-start.1 = ((f32[128,64,128]{2,1,0:T(8,128)}), f32[128,64,128]{2,1,0:T(8,128)}, u32[]{:S(2)}, u32[]{:S(2)}) async-start(f32[128,64,128]{2,1,0:T(8,128)} %slice.26), calls=%async_computation.2 | async-start | bytes 8388608 | tf_op jit(solution)/shard_map/all_to_all | solution.py:85
  241.3 0.7 all-gather.3.cloned.1.call-update
  242.1 1.0 slice.25
  243.1 50.4 %all-to-all-done.1 = f32[128,64,128]{2,1,0:T(8,128)} async-done(((f32[128,64,128]{2,1,0:T(8,128)}), f32[128,64,128]{2,1,0:T(8,128)}, u32[]{:S(2)}, u32[]{:S(2)}) %all-to-all-start.1) | async-done | bytes 4194336 | tf_op jit(solution)/shard_map/all_to_all | solution.py:85
  293.5 4.5 broadcast_multiply_fusion.2
  298.0 13.5 %scatter_fusion.2 = f32[8,64,128]{2,1,0:T(8,128)S(1)} fusion(f32[8,64,128]{2,1,0:T(8,128)S(1)} %slice.25, s32[128]{0:T(128)S(1)} %reshape_squeeze.5, f32[128,64,128]{2,1,0:T(8,128)} %broadcast_multiply_fusion.2), kind=kCustom, calls=%fused_computation.6 | custom fusion | flops 1048576 | bytes 12583424 | tf_op jit(solution)/shard_map/scatter-add | solution.py:90
  311.5 0.7 copy_bitcast_fusion.1
  312.3 2.2 convolution_bitcast_fusion.1
  314.5 29.7 %all-gather.5.cloned.1.call-done = bf16[512,1024]{1,0:T(8,128)(2,1)} async-done(((bf16[64,1024]{1,0:T(8,128)(2,1)}), bf16[512,1024]{1,0:T(8,128)(2,1)}) %all-gather.5.cloned.1.call-update) | async-done | bytes 1048592 | tf_op jit(solution)/shard_map/all_gather | solution.py:99
  344.2 2.2 convolution_bitcast_fusion
  346.5 112.6 %all-reduce.3.cloned.1.call-done = (f32[16,512]{1,0:T(8,128)}, f32[16,512]{1,0:T(8,128)}, f32[64]{0:T(128)}) async-done(((f32[16,512]{1,0:T(8,128)}, f32[16,512]{1,0:T(8,128)}, f32[64]{0:T(128)}), (f32[16,512]{1,0:T(8,128)}, f32[16,512]{1,0:T(8,128)}, f32[64]{0:T(128)})) %all-reduce.3.cloned.1.call-update) | async-done | bytes 65808 | tf_op jit(solution)/shard_map/psum | solution.py:105
  459.1 1.4 copy.120
  460.4 1.4 copy.121
  461.8 1.2 copy.122
  (50 shorter events, 4.7 us)
Async XLA Ops:
  7.2 0.8 copy-start
  7.2 1.9 copy-start.3
  7.2 64.2 %reduce-scatter.2.cloned.1.call-start = ((), (), s32[]{:S(2)}) async-start(), calls=%async_computation.3 | async-start | bytes 4718592 | tf_op jit(solution)/shard_map/reduce_scatter | solution.py:34
  12.0 0.7 copy-start.6
  12.0 1.0 copy-start.8
  93.8 8.3 %copy-start.4 = (s32[1,256]{1,0:T(1,128)S(1)}, s32[1,256]{1,0:T(1,128)}, u32[]{:S(2)}) copy-start(s32[1,256]{1,0:T(1,128)} %param.18) | copy-start | bytes 3076
  93.8 35.9 %all-to-all-start = ((bf16[32,64,512]{2,1,0:T(8,128)(2,1)}), bf16[32,64,512]{2,1,0:T(8,128)(2,1)S(1)}, u32[]{:S(2)}, u32[]{:S(2)}) async-start(bf16[32,64,512]{2,1,0:T(8,128)(2,1)} %fusion.37), calls=%async_computation.1 | async-start | bytes 4194304 | tf_op jit(solution)/shard_map/all_to_all | solution.py:45
  102.1 5.7 %copy-start.5 = (s32[1,256]{1,0:T(1,128)S(1)}, s32[1,256]{1,0:T(1,128)}, u32[]{:S(2)}) copy-start(s32[1,256]{1,0:T(1,128)} %param.17) | copy-start | bytes 3076
  102.1 8.0 %copy-start.1 = (f32[64,2048]{1,0:T(8,128)S(1)}, f32[64,2048]{1,0:T(8,128)}, u32[]{:S(2)}) copy-start(f32[64,2048]{1,0:T(8,128)} %reduce-scatter.2.cloned.1.call-done) | copy-start | bytes 1572868
  147.2 26.3 %copy-start.2 = (bf16[64,1024]{1,0:T(8,128)(2,1)S(1)}, bf16[64,1024]{1,0:T(8,128)(2,1)}, u32[]{:S(2)}) copy-start(bf16[64,1024]{1,0:T(8,128)(2,1)} %param.21) | copy-start | bytes 393220
  147.2 26.3 %copy-start.7 = (f32[64]{0:T(128)S(1)}, f32[64]{0:T(128)}, u32[]{:S(2)}) copy-start(f32[64]{0:T(128)} %param.14) | copy-start | bytes 772
  235.8 57.7 %all-to-all-start.1 = ((f32[128,64,128]{2,1,0:T(8,128)}), f32[128,64,128]{2,1,0:T(8,128)}, u32[]{:S(2)}, u32[]{:S(2)}) async-start(f32[128,64,128]{2,1,0:T(8,128)} %slice.26), calls=%async_computation.2 | async-start | bytes 8388608 | tf_op jit(solution)/shard_map/all_to_all | solution.py:85
  241.2 71.1 %all-gather.3.cloned.1.call-start = ((), (), s32[]{:S(2)}) async-start(), calls=%async_computation.4 | async-start | bytes 1179648 | tf_op jit(solution)/shard_map/all_gather | solution.py:98
  242.0 102.3 %all-gather.5.cloned.1.call-start = ((), (), s32[]{:S(2)}) async-start(), calls=%async_computation.5 | async-start | bytes 1179648 | tf_op jit(solution)/shard_map/all_gather | solution.py:99
  312.2 146.8 %all-reduce.3.cloned.1.call-start = ((), (), s32[]{:S(2)}) async-start(), calls=%async_computation.6 | async-start | bytes 132096 | tf_op jit(solution)/shard_map/psum | solution.py:105
Sparse Core Ops, SparseCore 0:
  12.2 59.1 reduce-scatter.1
  243.8 33.6 all-gather.2
  312.3 31.8 all-gather.4
  348.3 110.7 all-reduce.2
